TPU v7x, 768 devices: a whole 4x8x12 slice. The times are simulated.
768 devices in a mesh: gx: 16 (over y, x_hi), gy: 4 (over x_lo, core), gz: 12 (over z).
Axes of the slice: x: 4 (x_hi: 2, x_lo: 2; x = x_hi * 2 + x_lo), y: 8, z: 12, core: 2. Of those that a mesh axis runs over, the one named last changes fastest.
Arguments:
- flexibility: bfloat16 [16, 4, 12, 768, 768], P('gx', 'gy', 'gz'), may hold values from -6 to 6, as said below
- stiffness: bfloat16 [16, 4, 12, 768, 768], P('gx', 'gy', 'gz'), may hold values from -6 to 6, as said below
- local_load: float32 [16, 4, 12, 6, 128, 128], P('gx', 'gy', 'gz'), may hold values from -80 to 80
- face_map: int32 [16, 4, 12, 6, 128], P('gx', 'gy', 'gz'), may hold values from 0 to 127, each once within a row
- face_sign: int32 [16, 4, 12, 6, 128], P('gx', 'gy', 'gz'), may hold values from -1 to 1, as said below
Outputs:
- multipliers: float32 [16, 4, 12, 3, 128, 128], P('gx', 'gy', 'gz')
- residual: float32 [16, 4, 12, 3, 128, 128], P('gx', 'gy', 'gz')
Inputs may be any that keep to these rules, and one draw needn't show every extreme that they name: `face_map`: each row is a permutation of 0 to 127. `face_sign`: every entry is +1 or -1, and the two subdomains sharing a face give each of its multipliers opposite signs. `flexibility`: each subdomain's matrix is symmetric positive definite. `stiffness`: each subdomain's matrix is symmetric positive definite.
All inputs are finite; a program needn't handle non-finite values.
Results may differ from a plain program's by a relative error of at most 0.011.
Values sent between devices are 32-bit elements; how exact they have to be, the bound alone decides.
No kernel may reach another device: no remote copies, remote signals or barrier semaphores. Data moves between devices by JAX's collectives and lax.ppermute only.
A program may use at most 32 MiB of HBM per device.

v0:
```python
import jax
import jax.numpy as jnp
from jax import lax
from jax.sharding import Mesh
from jax.sharding import PartitionSpec as P

ITERS = 2
GX = ("gx_0", "gx_1")
GY = ("gy_0", "gy_1")
GX_GY_GZ = ("gx_0", "gx_1", "gy_0", "gy_1", "gz")


def with_halo(array, sides, width):
    for axis, dim in sides:
        count, length = (lax.axis_size(axis), array.shape[dim])
        up = [(i, (i + 1) % count) for i in range(count)]
        down = [(j, i) for i, j in up]
        last = lax.slice_in_dim(array, length - width, length, axis=dim)
        first = lax.slice_in_dim(array, 0, width, axis=dim)
        before = lax.ppermute(last, axis, up)
        after = lax.ppermute(first, axis, down)
        array = jnp.concatenate([before, array, after], axis=dim)
    return array


def by_axis(array, axes):
    for axis in axes:
        array = lax.psum(array, axis)
    return array


def assemble(vector):
    along_x = with_halo(vector[0:2], ((GX, 0),), 1)
    along_y = with_halo(vector[2:4], ((GY, 0),), 1)
    along_z = with_halo(vector[4:6], (("gz", 0),), 1)
    return jnp.stack(
        [
            vector[0] + along_x[0],
            vector[1] + along_x[3],
            vector[2] + along_y[0],
            vector[3] + along_y[3],
            vector[4] + along_z[0],
            vector[5] + along_z[3],
        ]
    )


def local_product(operator, face_rows, inverse, signs, vector):
    width = vector.shape[1]
    columns = vector.shape[2]
    signed = (signs * vector).reshape(6 * width, columns)
    restricted = signed[inverse].astype(jnp.bfloat16)
    product = jnp.dot(operator, restricted, preferred_element_type=jnp.float32)
    return signs * product[face_rows].reshape(6, width, columns)


def apply_operator(operator, face_rows, inverse, signs, vector):
    return assemble(local_product(operator, face_rows, inverse, signs, vector))


def inner_pair(residual, precond, image_z):
    gamma_part = jnp.sum(residual[0::2] * precond[0::2], axis=(0, 1))
    delta_part = jnp.sum(precond[0::2] * image_z[0::2], axis=(0, 1))
    return (by_axis(gamma_part, GX_GY_GZ), by_axis(delta_part, GX_GY_GZ))


def shards(flexibility, stiffness, local_load, face_map, face_sign):
    flex_local = flexibility[0, 0, 0]
    stiff_local = stiffness[0, 0, 0]
    width = face_map.shape[-1]
    maps_local = face_map[0, 0, 0]
    signs = face_sign[0, 0, 0].astype(jnp.float32)[:, :, None]
    face_rows = (jnp.arange(6, dtype=jnp.int32)[:, None] * width + maps_local).reshape(-1)
    inverse = (
        jnp.zeros((6 * width,), jnp.int32).at[face_rows].set(jnp.arange(6 * width, dtype=jnp.int32))
    )
    residual = assemble(local_load[0, 0, 0])
    multipliers = jnp.zeros_like(residual)
    precond = apply_operator(stiff_local, face_rows, inverse, signs, residual)
    image_z = apply_operator(flex_local, face_rows, inverse, signs, precond)
    gamma_now, delta_now = inner_pair(residual, precond, image_z)
    step_size = gamma_now / delta_now
    direction = precond
    image_dir = image_z
    for iteration in range(ITERS):
        multipliers = multipliers + step_size * direction
        residual = residual - step_size * image_dir
        if iteration + 1 < ITERS:
            precond = apply_operator(stiff_local, face_rows, inverse, signs, residual)
            image_z = apply_operator(flex_local, face_rows, inverse, signs, precond)
            gamma_new, delta_now = inner_pair(residual, precond, image_z)
            conjugacy = gamma_new / gamma_now
            step_size = gamma_new / (delta_now - conjugacy * gamma_new / step_size)
            direction = precond + conjugacy * direction
            image_dir = image_z + conjugacy * image_dir
            gamma_now = gamma_new
    return (multipliers[0::2][None, None, None], residual[0::2][None, None, None])


def solution(mesh):
    split = Mesh(
        mesh.devices.reshape(8, 2, 2, 2, mesh.shape["gz"]), ("gx_0", "gx_1", "gy_0", "gy_1", "gz")
    )
    placed = (
        P(GX, GY, "gz", None, None),
        P(GX, GY, "gz", None, None),
        P(GX, GY, "gz", None, None, None),
        P(GX, GY, "gz", None, None),
        P(GX, GY, "gz", None, None),
    )
    return jax.shard_map(
        shards,
        mesh=split,
        in_specs=placed,
        out_specs=(P(GX, GY, "gz", None, None, None), P(GX, GY, "gz", None, None, None)),
        check_vma=False,
    )
```

profile of v0, /device:TPU:2, one launch (start us, length us, event | category | flops | bytes accessed | tf_op | source)
XLA Modules:
  0.0 283.1 jit_solution(7169577811432410730)
XLA Ops:
  1.8 14.6 %collective-permute-start.5 = (f32[1,128,128]{2,1,0:T(8,128)S(1)}, f32[1,128,128]{2,1,0:T(8,128)S(1)}, u32[]{:S(2)}, u32[]{:S(2)}) collective-permute-start(f32[1,128,128]{2,1,0:T(8,128)S(1)} %get-tuple-element.52), channel_id=1, source_target_pairs={{1,0},{2,1},{3,2},{4,3},{5,4},{6,5},{7,6},{8,7},{9,8},{10,9},{11,1... | collective-permute-start | bytes 196616 | tf_op jit(solution)/shard_map/ppermute | solution.py:21
  16.4 1.9 collective-permute-start.2
  18.3 3.6 %collective-permute-start.3 = (f32[1,128,128]{2,1,0:T(8,128)S(1)}, f32[1,128,128]{2,1,0:T(8,128)S(1)}, u32[]{:S(2)}, u32[]{:S(2)}) collective-permute-start(f32[1,128,128]{2,1,0:T(8,128)S(1)} %get-tuple-element.54), channel_id=1, source_target_pairs={{12,0},{24,12},{36,24},{0,36},{13,1},{25,13},{37,25},{1,37},{14,2}... | collective-permute-start | bytes 196616 | tf_op jit(solution)/shard_map/ppermute | solution.py:21
  22.0 4.0 %collective-permute-start = (f32[1,128,128]{2,1,0:T(8,128)S(1)}, f32[1,128,128]{2,1,0:T(8,128)S(1)}, u32[]{:S(2)}, u32[]{:S(2)}) collective-permute-start(f32[1,128,128]{2,1,0:T(8,128)S(1)} %get-tuple-element.55), channel_id=1, source_target_pairs={{0,48},{48,96},{96,144},{144,192},{192,240},{240,288},{288,336},{3... | collective-permute-start | bytes 196616 | tf_op jit(solution)/shard_map/ppermute | solution.py:20
  26.0 5.4 %collective-permute-start.1 = (f32[1,128,128]{2,1,0:T(8,128)S(1)}, f32[1,128,128]{2,1,0:T(8,128)S(1)}, u32[]{:S(2)}, u32[]{:S(2)}) collective-permute-start(f32[1,128,128]{2,1,0:T(8,128)S(1)} %get-tuple-element.56), channel_id=1, source_target_pairs={{48,0},{96,48},{144,96},{192,144},{240,192},{288,240},{336,288},{3... | collective-permute-start | bytes 196616 | tf_op jit(solution)/shard_map/ppermute | solution.py:21
  33.7 3.4 %scatter_custom_fusion = s32[768]{0:T(1024)S(1)} fusion(s32[768]{0:T(1024)S(1)} %fusion.10, s32[768]{0:T(1024)S(1)} %iota.9, s32[]{:T(128)} %constant.0.clone.1), kind=kCustom, calls=%fused_computation.84 | custom fusion | bytes 3076 | tf_op jit(solution)/shard_map/scatter | solution.py:75
  37.1 1.9 collective-permute-start.4
  40.8 3.7 %collective-permute-done.4 = f32[1,128,128]{2,1,0:T(8,128)S(1)} collective-permute-done((f32[1,128,128]{2,1,0:T(8,128)S(1)}, f32[1,128,128]{2,1,0:T(8,128)S(1)}, u32[]{:S(2)}, u32[]{:S(2)}) %collective-permute-start.4) | collective-permute-done | bytes 65568 | tf_op jit(solution)/shard_map/ppermute | solution.py:20
  44.7 1.9 gather_fusion
  47.3 1.6 gather_fusion.1
  49.0 1.9 collective-permute-start.6
  51.0 7.8 %collective-permute-done.6 = f32[1,128,128]{2,1,0:T(8,128)S(1)} collective-permute-done((f32[1,128,128]{2,1,0:T(8,128)S(1)}, f32[1,128,128]{2,1,0:T(8,128)S(1)}, u32[]{:S(2)}, u32[]{:S(2)}) %collective-permute-start.6) | collective-permute-done | bytes 65568 | tf_op jit(solution)/shard_map/ppermute | solution.py:20
  58.8 2.7 collective-permute-start.7
  61.6 1.9 collective-permute-start.11
  63.5 3.9 %collective-permute-start.10 = (f32[1,128,128]{2,1,0:T(8,128)S(1)}, f32[1,128,128]{2,1,0:T(8,128)S(1)}, u32[]{:S(2)}, u32[]{:S(2)}) collective-permute-start(f32[1,128,128]{2,1,0:T(8,128)S(1)} %get-tuple-element.48), channel_id=1, source_target_pairs={{0,1},{1,2},{2,3},{3,4},{4,5},{5,6},{6,7},{7,8},{8,9},{9,10},{10,1... | collective-permute-start | bytes 196616 | tf_op jit(solution)/shard_map/ppermute | solution.py:20
  67.4 1.9 collective-permute-start.8
  69.3 3.6 %collective-permute-start.9 = (f32[1,128,128]{2,1,0:T(8,128)S(1)}, f32[1,128,128]{2,1,0:T(8,128)S(1)}, u32[]{:S(2)}, u32[]{:S(2)}) collective-permute-start(f32[1,128,128]{2,1,0:T(8,128)S(1)} %get-tuple-element.50), channel_id=1, source_target_pairs={{12,0},{24,12},{36,24},{0,36},{13,1},{25,13},{37,25},{1,37},{14,2}... | collective-permute-start | bytes 196616 | tf_op jit(solution)/shard_map/ppermute | solution.py:21
  73.0 1.8 collective-permute-done.9
  75.1 1.9 gather_fusion.2
  77.0 1.3 convolution_bitcast_fusion.2
  78.3 1.1 copy.8
  79.5 1.6 gather_fusion.3
  81.3 4.6 %collective-permute-start.12 = (f32[1,128,128]{2,1,0:T(8,128)S(1)}, f32[1,128,128]{2,1,0:T(8,128)S(1)}, u32[]{:S(2)}, u32[]{:S(2)}) collective-permute-start(f32[1,128,128]{2,1,0:T(8,128)S(1)} %slice.276), channel_id=1, source_target_pairs={{0,48},{48,96},{96,144},{144,192},{192,240},{240,288},{288,336},{3... | collective-permute-start | bytes 196616 | tf_op jit(solution)/shard_map/ppermute | solution.py:20
  85.9 5.2 %collective-permute-done.12 = f32[1,128,128]{2,1,0:T(8,128)S(1)} collective-permute-done((f32[1,128,128]{2,1,0:T(8,128)S(1)}, f32[1,128,128]{2,1,0:T(8,128)S(1)}, u32[]{:S(2)}, u32[]{:S(2)}) %collective-permute-start.12) | collective-permute-done | bytes 65568 | tf_op jit(solution)/shard_map/ppermute | solution.py:20
  91.1 2.9 %collective-permute-start.13 = (f32[1,128,128]{2,1,0:T(8,128)S(1)}, f32[1,128,128]{2,1,0:T(8,128)S(1)}, u32[]{:S(2)}, u32[]{:S(2)}) collective-permute-start(f32[1,128,128]{2,1,0:T(8,128)S(1)} %get-tuple-element.45), channel_id=1, source_target_pairs={{48,0},{96,48},{144,96},{192,144},{240,192},{288,240},{336,288},{3... | collective-permute-start | bytes 196616 | tf_op jit(solution)/shard_map/ppermute | solution.py:21
  94.1 3.1 %collective-permute-start.17 = (f32[1,128,128]{2,1,0:T(8,128)S(1)}, f32[1,128,128]{2,1,0:T(8,128)S(1)}, u32[]{:S(2)}, u32[]{:S(2)}) collective-permute-start(f32[1,128,128]{2,1,0:T(8,128)S(1)} %get-tuple-element.40), channel_id=1, source_target_pairs={{1,0},{2,1},{3,2},{4,3},{5,4},{6,5},{7,6},{8,7},{9,8},{10,9},{11,1... | collective-permute-start | bytes 196616 | tf_op jit(solution)/shard_map/ppermute | solution.py:21
  97.2 2.7 collective-permute-start.16
  99.9 1.9 collective-permute-start.14
  101.9 3.6 %collective-permute-start.15 = (f32[1,128,128]{2,1,0:T(8,128)S(1)}, f32[1,128,128]{2,1,0:T(8,128)S(1)}, u32[]{:S(2)}, u32[]{:S(2)}) collective-permute-start(f32[1,128,128]{2,1,0:T(8,128)S(1)} %get-tuple-element.44), channel_id=1, source_target_pairs={{12,0},{24,12},{36,24},{0,36},{13,1},{25,13},{37,25},{1,37},{14,2}... | collective-permute-start | bytes 196616 | tf_op jit(solution)/shard_map/ppermute | solution.py:21
  105.6 1.8 collective-permute-done.15
  107.6 17.4 %all-reduce.3 = (f32[128]{0:T(128)S(1)}, f32[128]{0:T(128)S(1)}) all-reduce(f32[128]{0:T(128)S(1)} %get-tuple-element.5, f32[128]{0:T(128)S(1)} %get-tuple-element.4), channel_id=1, replica_groups=mesh['gx_0'=8,'gx_1'=2,'gy_0'=2,'gy_1'=2,'gz'=12] {'gx_0'}, use_global_device_ids=true, to_apply=%region_2.0 | all-reduce | flops 256 | bytes 2048 | tf_op jit(solution)/shard_map/psum | solution.py:28
  125.0 6.4 %all-reduce.9 = (f32[128]{0:T(128)S(1)}, f32[128]{0:T(128)S(1)}) all-reduce(f32[128]{0:T(128)S(1)} %get-tuple-element.12, f32[128]{0:T(128)S(1)} %get-tuple-element.13), channel_id=1, replica_groups=mesh['gx_0'=8,'gx_1'=2,'gy_0'=2,'gy_1'=2,'gz'=12] {'gx_1'}, use_global_device_ids=true, to_apply=%region_3.0 | all-reduce | flops 256 | bytes 2048 | tf_op jit(solution)/shard_map/psum | solution.py:28
  131.4 4.9 %all-reduce.7 = (f32[128]{0:T(128)S(1)}, f32[128]{0:T(128)S(1)}) all-reduce(f32[128]{0:T(128)S(1)} %get-tuple-element.24, f32[128]{0:T(128)S(1)} %get-tuple-element.25), channel_id=1, replica_groups=mesh['gx_0'=8,'gx_1'=2,'gy_0'=2,'gy_1'=2,'gz'=12] {'gy_0'}, use_global_device_ids=true, to_apply=%region_4.0 | all-reduce | flops 256 | bytes 2048 | tf_op jit(solution)/shard_map/psum | solution.py:28
  136.3 2.5 all-reduce.5
  138.8 23.0 %all-reduce.1 = (f32[128]{0:T(128)S(1)}, f32[128]{0:T(128)S(1)}) all-reduce(f32[128]{0:T(128)S(1)} %get-tuple-element.16, f32[128]{0:T(128)S(1)} %get-tuple-element.17), channel_id=1, replica_groups=mesh['gx_0'=8,'gx_1'=2,'gy_0'=2,'gy_1'=2,'gz'=12] {'gz'}, use_global_device_ids=true, to_apply=%region_6.0 | all-reduce | flops 256 | bytes 2048 | tf_op jit(solution)/shard_map/psum | solution.py:28
  163.0 1.9 gather_fusion.4
  164.9 1.3 convolution_bitcast_fusion.1
  166.2 1.1 copy.9
  167.4 2.3 gather_fusion.5
  169.7 1.2 broadcast_multiply_fusion.1
  170.8 2.0 collective-permute-start.18
  172.9 7.8 %collective-permute-done.18 = f32[1,128,128]{2,1,0:T(8,128)S(1)} collective-permute-done((f32[1,128,128]{2,1,0:T(8,128)S(1)}, f32[1,128,128]{2,1,0:T(8,128)S(1)}, u32[]{:S(2)}, u32[]{:S(2)}) %collective-permute-start.18) | collective-permute-done | bytes 65568 | tf_op jit(solution)/shard_map/ppermute | solution.py:20
  180.7 2.3 collective-permute-start.19
  183.0 1.9 collective-permute-start.23
  184.9 3.9 %collective-permute-start.22 = (f32[1,128,128]{2,1,0:T(8,128)S(1)}, f32[1,128,128]{2,1,0:T(8,128)S(1)}, u32[]{:S(2)}, u32[]{:S(2)}) collective-permute-start(f32[1,128,128]{2,1,0:T(8,128)S(1)} %get-tuple-element.36), channel_id=1, source_target_pairs={{0,1},{1,2},{2,3},{3,4},{4,5},{5,6},{6,7},{7,8},{8,9},{9,10},{10,1... | collective-permute-start | bytes 196616 | tf_op jit(solution)/shard_map/ppermute | solution.py:20
  188.9 1.9 collective-permute-start.20
  190.8 3.6 %collective-permute-start.21 = (f32[1,128,128]{2,1,0:T(8,128)S(1)}, f32[1,128,128]{2,1,0:T(8,128)S(1)}, u32[]{:S(2)}, u32[]{:S(2)}) collective-permute-start(f32[1,128,128]{2,1,0:T(8,128)S(1)} %get-tuple-element.38), channel_id=1, source_target_pairs={{12,0},{24,12},{36,24},{0,36},{13,1},{25,13},{37,25},{1,37},{14,2}... | collective-permute-start | bytes 196616 | tf_op jit(solution)/shard_map/ppermute | solution.py:21
  194.5 1.8 collective-permute-done.21
  197.3 2.5 gather_fusion.6
  199.9 1.5 convolution_bitcast_fusion
  201.5 1.6 gather_fusion.7
  203.3 5.0 %collective-permute-start.24 = (f32[1,128,128]{2,1,0:T(8,128)S(1)}, f32[1,128,128]{2,1,0:T(8,128)S(1)}, u32[]{:S(2)}, u32[]{:S(2)}) collective-permute-start(f32[1,128,128]{2,1,0:T(8,128)S(1)} %slice.288), channel_id=1, source_target_pairs={{0,48},{48,96},{96,144},{144,192},{192,240},{240,288},{288,336},{3... | collective-permute-start | bytes 196616 | tf_op jit(solution)/shard_map/ppermute | solution.py:20
  208.3 5.2 %collective-permute-done.24 = f32[1,128,128]{2,1,0:T(8,128)S(1)} collective-permute-done((f32[1,128,128]{2,1,0:T(8,128)S(1)}, f32[1,128,128]{2,1,0:T(8,128)S(1)}, u32[]{:S(2)}, u32[]{:S(2)}) %collective-permute-start.24) | collective-permute-done | bytes 65568 | tf_op jit(solution)/shard_map/ppermute | solution.py:20
  213.6 2.1 collective-permute-start.25
  215.7 3.1 %collective-permute-start.29 = (f32[1,128,128]{2,1,0:T(8,128)S(1)}, f32[1,128,128]{2,1,0:T(8,128)S(1)}, u32[]{:S(2)}, u32[]{:S(2)}) collective-permute-start(f32[1,128,128]{2,1,0:T(8,128)S(1)} %get-tuple-element.28), channel_id=1, source_target_pairs={{1,0},{2,1},{3,2},{4,3},{5,4},{6,5},{7,6},{8,7},{9,8},{10,9},{11,1... | collective-permute-start | bytes 196616 | tf_op jit(solution)/shard_map/ppermute | solution.py:21
  218.8 2.7 collective-permute-start.28
  221.6 1.9 collective-permute-start.26
  223.5 3.6 %collective-permute-start.27 = (f32[1,128,128]{2,1,0:T(8,128)S(1)}, f32[1,128,128]{2,1,0:T(8,128)S(1)}, u32[]{:S(2)}, u32[]{:S(2)}) collective-permute-start(f32[1,128,128]{2,1,0:T(8,128)S(1)} %get-tuple-element.32), channel_id=1, source_target_pairs={{12,0},{24,12},{36,24},{0,36},{13,1},{25,13},{37,25},{1,37},{14,2}... | collective-permute-start | bytes 196616 | tf_op jit(solution)/shard_map/ppermute | solution.py:21
  227.2 1.8 collective-permute-done.27
  229.2 16.2 %all-reduce.2 = (f32[128]{0:T(128)S(1)}, f32[128]{0:T(128)S(1)}) all-reduce(f32[128]{0:T(128)S(1)} %get-tuple-element.3, f32[128]{0:T(128)S(1)} %get-tuple-element.2), channel_id=1, replica_groups=mesh['gx_0'=8,'gx_1'=2,'gy_0'=2,'gy_1'=2,'gz'=12] {'gx_0'}, use_global_device_ids=true, to_apply=%region_14.0 | all-reduce | flops 256 | bytes 2048 | tf_op jit(solution)/shard_map/psum | solution.py:28
  245.3 6.4 %all-reduce.8 = (f32[128]{0:T(128)S(1)}, f32[128]{0:T(128)S(1)}) all-reduce(f32[128]{0:T(128)S(1)} %get-tuple-element.10, f32[128]{0:T(128)S(1)} %get-tuple-element.11), channel_id=1, replica_groups=mesh['gx_0'=8,'gx_1'=2,'gy_0'=2,'gy_1'=2,'gz'=12] {'gx_1'}, use_global_device_ids=true, to_apply=%region_15.0 | all-reduce | flops 256 | bytes 2048 | tf_op jit(solution)/shard_map/psum | solution.py:28
  251.8 4.9 %all-reduce.6 = (f32[128]{0:T(128)S(1)}, f32[128]{0:T(128)S(1)}) all-reduce(f32[128]{0:T(128)S(1)} %get-tuple-element.22, f32[128]{0:T(128)S(1)} %get-tuple-element.23), channel_id=1, replica_groups=mesh['gx_0'=8,'gx_1'=2,'gy_0'=2,'gy_1'=2,'gz'=12] {'gy_0'}, use_global_device_ids=true, to_apply=%region_16.0 | all-reduce | flops 256 | bytes 2048 | tf_op jit(solution)/shard_map/psum | solution.py:28
  256.7 2.5 all-reduce.4
  259.1 23.0 %all-reduce = (f32[128]{0:T(128)S(1)}, f32[128]{0:T(128)S(1)}) all-reduce(f32[128]{0:T(128)S(1)} %get-tuple-element.14, f32[128]{0:T(128)S(1)} %get-tuple-element.15), channel_id=1, replica_groups=mesh['gx_0'=8,'gx_1'=2,'gy_0'=2,'gy_1'=2,'gz'=12] {'gz'}, use_global_device_ids=true, to_apply=%region_18.0 | all-reduce | flops 256 | bytes 2048 | tf_op jit(solution)/shard_map/psum | solution.py:28
  (111 shorter events, 10.5 us)
Async XLA Ops:
  0.6 45.9 %copy-start = (bf16[1,1,1,768,768]{4,3,2,1,0:T(8,128)(2,1)S(1)}, bf16[1,1,1,768,768]{4,3,2,1,0:T(8,128)(2,1)}, u32[]{:S(2)}) copy-start(bf16[1,1,1,768,768]{4,3,2,1,0:T(8,128)(2,1)} %param.6) | copy-start | bytes 3538948
  0.6 40.1 %copy-start.7 = (f32[1,1,1,6,128,128]{5,4,3,2,1,0:T(8,128)S(1)}, f32[1,1,1,6,128,128]{5,4,3,2,1,0:T(8,128)}, u32[]{:S(2)}) copy-start(f32[1,1,1,6,128,128]{5,4,3,2,1,0:T(8,128)} %param.7) | copy-start | bytes 1179652
  1.8 42.7 %collective-permute-start.5 = (f32[1,128,128]{2,1,0:T(8,128)S(1)}, f32[1,128,128]{2,1,0:T(8,128)S(1)}, u32[]{:S(2)}, u32[]{:S(2)}) collective-permute-start(f32[1,128,128]{2,1,0:T(8,128)S(1)} %get-tuple-element.52), channel_id=1, source_target_pairs={{1,0},{2,1},{3,2},{4,3},{5,4},{6,5},{7,6},{8,7},{9,8},{10,9},{11,1... | collective-permute-start | bytes 196616 | tf_op jit(solution)/shard_map/ppermute | solution.py:21
  16.4 24.3 %collective-permute-start.2 = (f32[1,128,128]{2,1,0:T(8,128)S(1)}, f32[1,128,128]{2,1,0:T(8,128)S(1)}, u32[]{:S(2)}, u32[]{:S(2)}) collective-permute-start(f32[1,128,128]{2,1,0:T(8,128)S(1)} %get-tuple-element.53), channel_id=1, source_target_pairs={{0,12},{12,24},{24,36},{36,0},{1,13},{13,25},{25,37},{37,1},{2,14}... | collective-permute-start | bytes 196616 | tf_op jit(solution)/shard_map/ppermute | solution.py:20
  18.3 22.4 %collective-permute-start.3 = (f32[1,128,128]{2,1,0:T(8,128)S(1)}, f32[1,128,128]{2,1,0:T(8,128)S(1)}, u32[]{:S(2)}, u32[]{:S(2)}) collective-permute-start(f32[1,128,128]{2,1,0:T(8,128)S(1)} %get-tuple-element.54), channel_id=1, source_target_pairs={{12,0},{24,12},{36,24},{0,36},{13,1},{25,13},{37,25},{1,37},{14,2}... | collective-permute-start | bytes 196616 | tf_op jit(solution)/shard_map/ppermute | solution.py:21
  22.0 15.1 %collective-permute-start = (f32[1,128,128]{2,1,0:T(8,128)S(1)}, f32[1,128,128]{2,1,0:T(8,128)S(1)}, u32[]{:S(2)}, u32[]{:S(2)}) collective-permute-start(f32[1,128,128]{2,1,0:T(8,128)S(1)} %get-tuple-element.55), channel_id=1, source_target_pairs={{0,48},{48,96},{96,144},{144,192},{192,240},{240,288},{288,336},{3... | collective-permute-start | bytes 196616 | tf_op jit(solution)/shard_map/ppermute | solution.py:20
  26.0 13.8 %collective-permute-start.1 = (f32[1,128,128]{2,1,0:T(8,128)S(1)}, f32[1,128,128]{2,1,0:T(8,128)S(1)}, u32[]{:S(2)}, u32[]{:S(2)}) collective-permute-start(f32[1,128,128]{2,1,0:T(8,128)S(1)} %get-tuple-element.56), channel_id=1, source_target_pairs={{48,0},{96,48},{144,96},{192,144},{240,192},{288,240},{336,288},{3... | collective-permute-start | bytes 196616 | tf_op jit(solution)/shard_map/ppermute | solution.py:21
  37.1 7.4 %collective-permute-start.4 = (f32[1,128,128]{2,1,0:T(8,128)S(1)}, f32[1,128,128]{2,1,0:T(8,128)S(1)}, u32[]{:S(2)}, u32[]{:S(2)}) collective-permute-start(f32[1,128,128]{2,1,0:T(8,128)S(1)} %get-tuple-element.57), channel_id=1, source_target_pairs={{0,1},{1,2},{2,3},{3,4},{4,5},{5,6},{6,7},{7,8},{8,9},{9,10},{10,1... | collective-permute-start | bytes 196616 | tf_op jit(solution)/shard_map/ppermute | solution.py:20
  49.0 9.8 %collective-permute-start.6 = (f32[1,128,128]{2,1,0:T(8,128)S(1)}, f32[1,128,128]{2,1,0:T(8,128)S(1)}, u32[]{:S(2)}, u32[]{:S(2)}) collective-permute-start(f32[1,128,128]{2,1,0:T(8,128)S(1)} %slice.270), channel_id=1, source_target_pairs={{0,48},{48,96},{96,144},{144,192},{192,240},{240,288},{288,336},{3... | collective-permute-start | bytes 196616 | tf_op jit(solution)/shard_map/ppermute | solution.py:20
  58.8 14.2 %collective-permute-start.7 = (f32[1,128,128]{2,1,0:T(8,128)S(1)}, f32[1,128,128]{2,1,0:T(8,128)S(1)}, u32[]{:S(2)}, u32[]{:S(2)}) collective-permute-start(f32[1,128,128]{2,1,0:T(8,128)S(1)} %get-tuple-element.51), channel_id=1, source_target_pairs={{48,0},{96,48},{144,96},{192,144},{240,192},{288,240},{336,288},{3... | collective-permute-start | bytes 196616 | tf_op jit(solution)/shard_map/ppermute | solution.py:21
  61.6 13.4 %collective-permute-start.11 = (f32[1,128,128]{2,1,0:T(8,128)S(1)}, f32[1,128,128]{2,1,0:T(8,128)S(1)}, u32[]{:S(2)}, u32[]{:S(2)}) collective-permute-start(f32[1,128,128]{2,1,0:T(8,128)S(1)} %get-tuple-element.46), channel_id=1, source_target_pairs={{1,0},{2,1},{3,2},{4,3},{5,4},{6,5},{7,6},{8,7},{9,8},{10,9},{11,1... | collective-permute-start | bytes 196616 | tf_op jit(solution)/shard_map/ppermute | solution.py:21
  63.5 11.4 %collective-permute-start.10 = (f32[1,128,128]{2,1,0:T(8,128)S(1)}, f32[1,128,128]{2,1,0:T(8,128)S(1)}, u32[]{:S(2)}, u32[]{:S(2)}) collective-permute-start(f32[1,128,128]{2,1,0:T(8,128)S(1)} %get-tuple-element.48), channel_id=1, source_target_pairs={{0,1},{1,2},{2,3},{3,4},{4,5},{5,6},{6,7},{7,8},{8,9},{9,10},{10,1... | collective-permute-start | bytes 196616 | tf_op jit(solution)/shard_map/ppermute | solution.py:20
  67.4 5.6 %collective-permute-start.8 = (f32[1,128,128]{2,1,0:T(8,128)S(1)}, f32[1,128,128]{2,1,0:T(8,128)S(1)}, u32[]{:S(2)}, u32[]{:S(2)}) collective-permute-start(f32[1,128,128]{2,1,0:T(8,128)S(1)} %get-tuple-element.49), channel_id=1, source_target_pairs={{0,12},{12,24},{24,36},{36,0},{1,13},{13,25},{25,37},{37,1},{2,14}... | collective-permute-start | bytes 196616 | tf_op jit(solution)/shard_map/ppermute | solution.py:20
  69.3 5.5 %collective-permute-start.9 = (f32[1,128,128]{2,1,0:T(8,128)S(1)}, f32[1,128,128]{2,1,0:T(8,128)S(1)}, u32[]{:S(2)}, u32[]{:S(2)}) collective-permute-start(f32[1,128,128]{2,1,0:T(8,128)S(1)} %get-tuple-element.50), channel_id=1, source_target_pairs={{12,0},{24,12},{36,24},{0,36},{13,1},{25,13},{37,25},{1,37},{14,2}... | collective-permute-start | bytes 196616 | tf_op jit(solution)/shard_map/ppermute | solution.py:21
  74.9 2.1 copy-start.2
  75.0 2.1 copy-start.1
  81.1 26.4 %copy-start.3 = (f32[6,128,128]{2,1,0:T(8,128)S(1)}, f32[6,128,128]{2,1,0:T(8,128)}, u32[]{:S(2)}) copy-start(f32[6,128,128]{2,1,0:T(8,128)} %copy-done.2) | copy-start | bytes 1179652
  81.3 9.8 %collective-permute-start.12 = (f32[1,128,128]{2,1,0:T(8,128)S(1)}, f32[1,128,128]{2,1,0:T(8,128)S(1)}, u32[]{:S(2)}, u32[]{:S(2)}) collective-permute-start(f32[1,128,128]{2,1,0:T(8,128)S(1)} %slice.276), channel_id=1, source_target_pairs={{0,48},{48,96},{96,144},{144,192},{192,240},{240,288},{288,336},{3... | collective-permute-start | bytes 196616 | tf_op jit(solution)/shard_map/ppermute | solution.py:20
  91.1 14.4 %collective-permute-start.13 = (f32[1,128,128]{2,1,0:T(8,128)S(1)}, f32[1,128,128]{2,1,0:T(8,128)S(1)}, u32[]{:S(2)}, u32[]{:S(2)}) collective-permute-start(f32[1,128,128]{2,1,0:T(8,128)S(1)} %get-tuple-element.45), channel_id=1, source_target_pairs={{48,0},{96,48},{144,96},{192,144},{240,192},{288,240},{336,288},{3... | collective-permute-start | bytes 196616 | tf_op jit(solution)/shard_map/ppermute | solution.py:21
  94.1 13.4 %collective-permute-start.17 = (f32[1,128,128]{2,1,0:T(8,128)S(1)}, f32[1,128,128]{2,1,0:T(8,128)S(1)}, u32[]{:S(2)}, u32[]{:S(2)}) collective-permute-start(f32[1,128,128]{2,1,0:T(8,128)S(1)} %get-tuple-element.40), channel_id=1, source_target_pairs={{1,0},{2,1},{3,2},{4,3},{5,4},{6,5},{7,6},{8,7},{9,8},{10,9},{11,1... | collective-permute-start | bytes 196616 | tf_op jit(solution)/shard_map/ppermute | solution.py:21
  97.2 10.2 %collective-permute-start.16 = (f32[1,128,128]{2,1,0:T(8,128)S(1)}, f32[1,128,128]{2,1,0:T(8,128)S(1)}, u32[]{:S(2)}, u32[]{:S(2)}) collective-permute-start(f32[1,128,128]{2,1,0:T(8,128)S(1)} %get-tuple-element.42), channel_id=1, source_target_pairs={{0,1},{1,2},{2,3},{3,4},{4,5},{5,6},{6,7},{7,8},{8,9},{9,10},{10,1... | collective-permute-start | bytes 196616 | tf_op jit(solution)/shard_map/ppermute | solution.py:20
  99.9 5.6 %collective-permute-start.14 = (f32[1,128,128]{2,1,0:T(8,128)S(1)}, f32[1,128,128]{2,1,0:T(8,128)S(1)}, u32[]{:S(2)}, u32[]{:S(2)}) collective-permute-start(f32[1,128,128]{2,1,0:T(8,128)S(1)} %get-tuple-element.43), channel_id=1, source_target_pairs={{0,12},{12,24},{24,36},{36,0},{1,13},{13,25},{25,37},{37,1},{2,14}... | collective-permute-start | bytes 196616 | tf_op jit(solution)/shard_map/ppermute | solution.py:20
  101.9 5.5 %collective-permute-start.15 = (f32[1,128,128]{2,1,0:T(8,128)S(1)}, f32[1,128,128]{2,1,0:T(8,128)S(1)}, u32[]{:S(2)}, u32[]{:S(2)}) collective-permute-start(f32[1,128,128]{2,1,0:T(8,128)S(1)} %get-tuple-element.44), channel_id=1, source_target_pairs={{12,0},{24,12},{36,24},{0,36},{13,1},{25,13},{37,25},{1,37},{14,2}... | collective-permute-start | bytes 196616 | tf_op jit(solution)/shard_map/ppermute | solution.py:21
  161.8 0.6 copy-start.10
  161.8 0.6 copy-start.12
  162.4 0.5 copy-start.8
  170.8 9.8 %collective-permute-start.18 = (f32[1,128,128]{2,1,0:T(8,128)S(1)}, f32[1,128,128]{2,1,0:T(8,128)S(1)}, u32[]{:S(2)}, u32[]{:S(2)}) collective-permute-start(f32[1,128,128]{2,1,0:T(8,128)S(1)} %slice.282), channel_id=1, source_target_pairs={{0,48},{48,96},{96,144},{144,192},{192,240},{240,288},{288,336},{3... | collective-permute-start | bytes 196616 | tf_op jit(solution)/shard_map/ppermute | solution.py:20
  180.7 13.7 %collective-permute-start.19 = (f32[1,128,128]{2,1,0:T(8,128)S(1)}, f32[1,128,128]{2,1,0:T(8,128)S(1)}, u32[]{:S(2)}, u32[]{:S(2)}) collective-permute-start(f32[1,128,128]{2,1,0:T(8,128)S(1)} %get-tuple-element.39), channel_id=1, source_target_pairs={{48,0},{96,48},{144,96},{192,144},{240,192},{288,240},{336,288},{3... | collective-permute-start | bytes 196616 | tf_op jit(solution)/shard_map/ppermute | solution.py:21
  183.0 13.4 %collective-permute-start.23 = (f32[1,128,128]{2,1,0:T(8,128)S(1)}, f32[1,128,128]{2,1,0:T(8,128)S(1)}, u32[]{:S(2)}, u32[]{:S(2)}) collective-permute-start(f32[1,128,128]{2,1,0:T(8,128)S(1)} %get-tuple-element.34), channel_id=1, source_target_pairs={{1,0},{2,1},{3,2},{4,3},{5,4},{6,5},{7,6},{8,7},{9,8},{10,9},{11,1... | collective-permute-start | bytes 196616 | tf_op jit(solution)/shard_map/ppermute | solution.py:21
  184.9 11.4 %collective-permute-start.22 = (f32[1,128,128]{2,1,0:T(8,128)S(1)}, f32[1,128,128]{2,1,0:T(8,128)S(1)}, u32[]{:S(2)}, u32[]{:S(2)}) collective-permute-start(f32[1,128,128]{2,1,0:T(8,128)S(1)} %get-tuple-element.36), channel_id=1, source_target_pairs={{0,1},{1,2},{2,3},{3,4},{4,5},{5,6},{6,7},{7,8},{8,9},{9,10},{10,1... | collective-permute-start | bytes 196616 | tf_op jit(solution)/shard_map/ppermute | solution.py:20
  188.9 5.6 %collective-permute-start.20 = (f32[1,128,128]{2,1,0:T(8,128)S(1)}, f32[1,128,128]{2,1,0:T(8,128)S(1)}, u32[]{:S(2)}, u32[]{:S(2)}) collective-permute-start(f32[1,128,128]{2,1,0:T(8,128)S(1)} %get-tuple-element.37), channel_id=1, source_target_pairs={{0,12},{12,24},{24,36},{36,0},{1,13},{13,25},{25,37},{37,1},{2,14}... | collective-permute-start | bytes 196616 | tf_op jit(solution)/shard_map/ppermute | solution.py:20
  190.8 5.5 %collective-permute-start.21 = (f32[1,128,128]{2,1,0:T(8,128)S(1)}, f32[1,128,128]{2,1,0:T(8,128)S(1)}, u32[]{:S(2)}, u32[]{:S(2)}) collective-permute-start(f32[1,128,128]{2,1,0:T(8,128)S(1)} %get-tuple-element.38), channel_id=1, source_target_pairs={{12,0},{24,12},{36,24},{0,36},{13,1},{25,13},{37,25},{1,37},{14,2}... | collective-permute-start | bytes 196616 | tf_op jit(solution)/shard_map/ppermute | solution.py:21
  196.4 0.8 copy-start.5
  203.1 12.6 %copy-start.9 = (f32[128]{0:T(128)S(1)}, f32[128]{0:T(128)}, u32[]{:S(2)}) copy-start(f32[128]{0:T(128)} %copy-done.8) | copy-start | bytes 1540
  203.3 10.3 %collective-permute-start.24 = (f32[1,128,128]{2,1,0:T(8,128)S(1)}, f32[1,128,128]{2,1,0:T(8,128)S(1)}, u32[]{:S(2)}, u32[]{:S(2)}) collective-permute-start(f32[1,128,128]{2,1,0:T(8,128)S(1)} %slice.288), channel_id=1, source_target_pairs={{0,48},{48,96},{96,144},{144,192},{192,240},{240,288},{288,336},{3... | collective-permute-start | bytes 196616 | tf_op jit(solution)/shard_map/ppermute | solution.py:20
  213.5 15.6 %copy-start.6 = (f32[6,128,128]{2,1,0:T(8,128)S(1)}, f32[6,128,128]{2,1,0:T(8,128)}, u32[]{:S(2)}) copy-start(f32[6,128,128]{2,1,0:T(8,128)} %copy-done.5) | copy-start | bytes 1179652
  213.6 68.6 %copy-start.11 = (f32[128]{0:T(128)S(1)}, f32[128]{0:T(128)}, u32[]{:S(2)}) copy-start(f32[128]{0:T(128)} %copy-done.10) | copy-start | bytes 1540
  213.6 68.6 %copy-start.13 = (f32[128]{0:T(128)S(1)}, f32[128]{0:T(128)}, u32[]{:S(2)}) copy-start(f32[128]{0:T(128)} %copy-done.12) | copy-start | bytes 1540
  213.6 68.6 %copy-start.4 = (f32[6,128,128]{2,1,0:T(8,128)S(1)}, f32[6,128,128]{2,1,0:T(8,128)}, u32[]{:S(2)}) copy-start(f32[6,128,128]{2,1,0:T(8,128)} %copy-done.2) | copy-start | bytes 1179652
  213.6 13.6 %collective-permute-start.25 = (f32[1,128,128]{2,1,0:T(8,128)S(1)}, f32[1,128,128]{2,1,0:T(8,128)S(1)}, u32[]{:S(2)}, u32[]{:S(2)}) collective-permute-start(f32[1,128,128]{2,1,0:T(8,128)S(1)} %get-tuple-element.33), channel_id=1, source_target_pairs={{48,0},{96,48},{144,96},{192,144},{240,192},{288,240},{336,288},{3... | collective-permute-start | bytes 196616 | tf_op jit(solution)/shard_map/ppermute | solution.py:21
  215.7 13.4 %collective-permute-start.29 = (f32[1,128,128]{2,1,0:T(8,128)S(1)}, f32[1,128,128]{2,1,0:T(8,128)S(1)}, u32[]{:S(2)}, u32[]{:S(2)}) collective-permute-start(f32[1,128,128]{2,1,0:T(8,128)S(1)} %get-tuple-element.28), channel_id=1, source_target_pairs={{1,0},{2,1},{3,2},{4,3},{5,4},{6,5},{7,6},{8,7},{9,8},{10,9},{11,1... | collective-permute-start | bytes 196616 | tf_op jit(solution)/shard_map/ppermute | solution.py:21
  218.8 10.2 %collective-permute-start.28 = (f32[1,128,128]{2,1,0:T(8,128)S(1)}, f32[1,128,128]{2,1,0:T(8,128)S(1)}, u32[]{:S(2)}, u32[]{:S(2)}) collective-permute-start(f32[1,128,128]{2,1,0:T(8,128)S(1)} %get-tuple-element.30), channel_id=1, source_target_pairs={{0,1},{1,2},{2,3},{3,4},{4,5},{5,6},{6,7},{7,8},{8,9},{9,10},{10,1... | collective-permute-start | bytes 196616 | tf_op jit(solution)/shard_map/ppermute | solution.py:20
  221.6 5.6 %collective-permute-start.26 = (f32[1,128,128]{2,1,0:T(8,128)S(1)}, f32[1,128,128]{2,1,0:T(8,128)S(1)}, u32[]{:S(2)}, u32[]{:S(2)}) collective-permute-start(f32[1,128,128]{2,1,0:T(8,128)S(1)} %get-tuple-element.31), channel_id=1, source_target_pairs={{0,12},{12,24},{24,36},{36,0},{1,13},{13,25},{25,37},{37,1},{2,14}... | collective-permute-start | bytes 196616 | tf_op jit(solution)/shard_map/ppermute | solution.py:20
  223.5 5.5 %collective-permute-start.27 = (f32[1,128,128]{2,1,0:T(8,128)S(1)}, f32[1,128,128]{2,1,0:T(8,128)S(1)}, u32[]{:S(2)}, u32[]{:S(2)}) collective-permute-start(f32[1,128,128]{2,1,0:T(8,128)S(1)} %get-tuple-element.32), channel_id=1, source_target_pairs={{12,0},{24,12},{36,24},{0,36},{13,1},{25,13},{37,25},{1,37},{14,2}... | collective-permute-start | bytes 196616 | tf_op jit(solution)/shard_map/ppermute | solution.py:21
where the time goes:
time: 285 us; the launch traced here: 283 us
  blocking collectives  107 us (38%)
  starting transfers between devices  101 us (35%)
  waiting for transfers between devices  37.1 us (13%)
  local copies, waits for them, and re-layouts  25.1 us (9%)
  other arithmetic  6.82 us (2%)
  matrix products  4.55 us (2%)
    psum x10, blocking collectives, by_axis(): array = lax.psum(array, axis)  107 us
    ppermute x15, starting transfers between devices, with_halo(): after = lax.ppermute(first, axis, down)  58.3 us
    ppermute x15, starting transfers between devices, with_halo(): before = lax.ppermute(last, axis, up)  42.5 us
    ppermute x15, waiting for transfers between devices, with_halo(): before = lax.ppermute(last, axis, up)  29.7 us
    gather x4, local copies, waits for them, and re-layouts, local_product(): restricted = signed[inverse].astype(jnp.bfloat16)  8.18 us
    ppermute x15, waiting for transfers between devices, with_halo(): after = lax.ppermute(first, axis, down)  7.34 us
    gather x4, local copies, waits for them, and re-layouts, local_product(): return signs * product[face_rows].reshape(6, width, columns)  7 us
  transfers between devices with their start and end apart: 30, of which 9 were waited for; matrix products, arithmetic and copies ran while one was open for 3% of the time, Pallas kernels for 0%

commit v1 on v0

v1 whole, which is shorter than its diff:
```python
import jax
import jax.numpy as jnp
from jax import lax
from jax.experimental import pallas as pl
from jax.experimental.pallas import tpu as pltpu
from jax.sharding import Mesh
from jax.sharding import PartitionSpec as P

GX = ("gx_0", "gx_1")
GY = ("gy_0", "gy_1")
GZ = ("gz",)
AXES = (GX, GY, GZ)
FACES = 6
VMEM_LIMIT = 16 * 2**20


def shift(array, axis, step):
    count = lax.axis_size(axis)
    pairs = [(i, (i + step) % count) for i in range(count)]
    return lax.ppermute(array, axis, pairs)


def exchange(faces):
    across = [None] * FACES
    for dim, axis in enumerate(AXES):
        across[2 * dim] = shift(faces[2 * dim + 1], axis, 1)
        across[2 * dim + 1] = shift(faces[2 * dim], axis, -1)
    return across


def exchange_up(faces):
    across = []
    for dim, axis in enumerate(AXES):
        across.append(shift(faces[2 * dim + 1], axis, 1))
    return across


def vmem_spec():
    return pl.BlockSpec(memory_space=pltpu.VMEM)


def on_chip(arrays):
    return [pltpu.with_memory_space_constraint(array, pltpu.VMEM) for array in arrays]


def reorder_body(operator_ref, map_ref, sign_ref, out_ref, half_ref):
    width = map_ref.shape[1]
    rows = lax.broadcasted_iota(jnp.int32, (width, width), 0)
    select = []
    for face in range(FACES):
        hit = rows == map_ref[face : face + 1, :]
        signs = sign_ref[face : face + 1, :].astype(jnp.float32)
        select.append(jnp.where(hit, jnp.broadcast_to(signs, (width, width)), 0.0))
    for face in range(FACES):
        span = slice(face * width, (face + 1) * width)
        half_ref[:, span] = jnp.dot(
            operator_ref[:, span],
            select[face].astype(jnp.bfloat16),
            preferred_element_type=jnp.float32,
        ).astype(jnp.bfloat16)
    for face in range(FACES):
        span = slice(face * width, (face + 1) * width)
        out_ref[span, :] = jnp.dot(
            select[face].T.astype(jnp.bfloat16),
            half_ref[span, :],
            preferred_element_type=jnp.float32,
        ).astype(jnp.bfloat16)


def reorder(operator, maps, signs):
    order = operator.shape[0]
    return pl.pallas_call(
        reorder_body,
        out_shape=pltpu.VMEM((order, order), jnp.bfloat16),
        in_specs=[vmem_spec()] * 3,
        out_specs=vmem_spec(),
        scratch_shapes=[pltpu.VMEM((order, order), jnp.bfloat16)],
        compiler_params=pltpu.CompilerParams(vmem_limit_bytes=VMEM_LIMIT),
        name="reorder",
    )(operator, maps, signs)


def product_body(*refs):
    operator_ref = refs[0]
    own = refs[1 : 1 + FACES]
    across = refs[1 + FACES : 1 + 2 * FACES]
    outs = refs[1 + 2 * FACES :]
    local = outs[:FACES]
    dot_ref = outs[FACES]
    kept = outs[FACES + 1]
    width = own[0].shape[0]
    full = [own[face][...] + across[face][...] for face in range(FACES)]
    for dim in range(3):
        kept[dim] = full[2 * dim]
    full = jnp.concatenate(full, axis=0)
    high = full.astype(jnp.bfloat16)
    low = (full - high.astype(jnp.float32)).astype(jnp.bfloat16)
    both = jnp.concatenate([high, low], axis=1)
    result = jnp.dot(operator_ref[...], both, preferred_element_type=jnp.float32)
    columns = full.shape[1]
    result = result[:, :columns] + result[:, columns:]
    for face in range(FACES):
        local[face][...] = result[face * width : (face + 1) * width, :]
    dot_ref[...] = jnp.sum(full * result, axis=0, keepdims=True)


def product(operator, own, across):
    width, columns = own[0].shape
    face = pltpu.VMEM((width, columns), jnp.float32)
    outs = pl.pallas_call(
        product_body,
        out_shape=[face] * FACES
        + [
            pltpu.VMEM((1, columns), jnp.float32),
            pltpu.VMEM((3, width, columns), jnp.float32),
        ],
        in_specs=[vmem_spec()] * (1 + 2 * FACES),
        out_specs=[vmem_spec()] * (FACES + 2),
        compiler_params=pltpu.CompilerParams(vmem_limit_bytes=VMEM_LIMIT),
        name="product",
    )(*on_chip([operator, *own, *across]))
    return outs[:FACES], outs[FACES], outs[FACES + 1]


def finish_body(sums_ref, r0_ref, z0_ref, w0_ref, u_ref, v0, v2, v4, a0, a2, a4, mult_ref, res_ref):
    gamma = sums_ref[0:1, :]
    delta = sums_ref[1:2, :]
    eps = sums_ref[2:3, :]
    zeta = sums_ref[3:4, :]
    step = gamma / delta
    gamma_new = step * (step * eps) - gamma
    delta_new = delta - 2.0 * (step * eps) + step * (step * zeta)
    beta = gamma_new / gamma
    step_new = gamma_new / (delta_new - beta * gamma_new / step)
    first = step + step_new * (1.0 + beta)
    second = step_new * step
    for dim, (own, across) in enumerate(((v0, a0), (v2, a2), (v4, a4))):
        mult_ref[dim] = first * z0_ref[dim] - second * u_ref[dim]
        image = own[...] + across[...]
        res_ref[dim] = r0_ref[dim] - first * w0_ref[dim] + second * image


def finish(sums, r0, z0, w0, u, own, across):
    shape = jax.ShapeDtypeStruct(r0.shape, jnp.float32)
    return pl.pallas_call(
        finish_body,
        out_shape=[shape, shape],
        in_specs=[vmem_spec()] * 11,
        out_specs=[vmem_spec()] * 2,
        compiler_params=pltpu.CompilerParams(vmem_limit_bytes=VMEM_LIMIT),
        name="finish",
    )(*on_chip([sums, r0, z0, w0, u, own[0], own[2], own[4], *across]))


def total(parts):
    for group in (GY + GZ, GX):
        count = lax.axis_size(group)
        spread = jnp.broadcast_to(parts[None], (count,) + parts.shape)
        parts = jnp.sum(lax.all_to_all(spread, group, 0, 0), axis=0)
    return parts


def shards(flexibility, stiffness, local_load, face_map, face_sign):
    maps = face_map[0, 0, 0]
    signs = face_sign[0, 0, 0]
    load = local_load[0, 0, 0]
    own = [load[face] for face in range(FACES)]
    across = exchange(own)
    stiff = reorder(stiffness[0, 0, 0], maps, signs)
    flex = reorder(flexibility[0, 0, 0], maps, signs)
    own, gamma, r0 = product(stiff, own, across)
    own, delta, z0 = product(flex, own, exchange(own))
    own, eps, w0 = product(stiff, own, exchange(own))
    own, zeta, u = product(flex, own, exchange(own))
    across = exchange_up(own)
    sums = total(jnp.concatenate([gamma, delta, eps, zeta], axis=0))
    mult, res = finish(sums, r0, z0, w0, u, own, across)
    return mult[None, None, None], res[None, None, None]


def solution(mesh):
    split = Mesh(
        mesh.devices.reshape(mesh.shape["gx"] // 2, 2, mesh.shape["gy"] // 2, 2, mesh.shape["gz"]),
        ("gx_0", "gx_1", "gy_0", "gy_1", "gz"),
    )
    vector = P(GX, GY, "gz", None, None, None)
    matrix = P(GX, GY, "gz", None, None)
    return jax.shard_map(
        shards,
        mesh=split,
        in_specs=(matrix, matrix, vector, matrix, matrix),
        out_specs=(vector, vector),
        check_vma=False,
    )
```

time: 285 us -> 148 us (0.52)
  the two profiles are of different devices: /device:TPU:2 before, /device:TPU:1 now
where the time goes in v1:
time: 148 us; the launch traced here: 147 us
  starting transfers between devices  106 us (72%)
  blocking collectives  16.7 us (11%)
  waiting for transfers between devices  15 us (10%)
  Pallas kernels  4.39 us (3%)
  local copies, waits for them, and re-layouts  3.67 us (2%)
    ppermute x27, starting transfers between devices, shift(): return lax.ppermute(array, axis, pairs)  99.9 us
    all_to_all x1, blocking collectives, total(): parts = jnp.sum(lax.all_to_all(spread, group, 0, 0), axis=0)  16.7 us
    ppermute x27, waiting for transfers between devices, shift(): return lax.ppermute(array, axis, pairs)  11 us
    all_to_all x1, starting transfers between devices, total(): parts = jnp.sum(lax.all_to_all(spread, group, 0, 0), axis=0)  5.71 us
    all_to_all x1, waiting for transfers between devices, total(): parts = jnp.sum(lax.all_to_all(spread, group, 0, 0), axis=0)  4.01 us
  transfers between devices with their start and end apart: 28, of which 6 were waited for; matrix products, arithmetic and copies ran while one was open for 1% of the time, Pallas kernels for 1%

profile of v1, /device:TPU:1, one launch (start us, length us, event | category | flops | bytes accessed | tf_op | source)
XLA Modules:
  0.0 146.7 jit_solution(4987202931739380453)
XLA Ops:
  0.6 1.0 slice_bitcast_fusion
  1.7 4.8 %collective-permute-start.4 = (f32[128,128]{1,0:T(8,128)S(1)}, f32[128,128]{1,0:T(8,128)S(1)}, u32[]{:S(2)}, u32[]{:S(2)}) collective-permute-start(f32[128,128]{1,0:T(8,128)S(1)} %get-tuple-element.70.refs_6_), channel_id=1, source_target_pairs={{0,1},{1,2},{2,3},{3,4},{4,5},{5,6},{6,7},{7,8},{8,9},{9,10},{10,1... | collective-permute-start | bytes 196616 | tf_op jit(solution)/shard_map/ppermute | solution.py:20
  6.5 4.0 %collective-permute-start.2 = (f32[128,128]{1,0:T(8,128)S(1)}, f32[128,128]{1,0:T(8,128)S(1)}, u32[]{:S(2)}, u32[]{:S(2)}) collective-permute-start(f32[128,128]{1,0:T(8,128)S(1)} %get-tuple-element.71.refs_4_), channel_id=1, source_target_pairs={{0,12},{12,24},{24,36},{36,0},{1,13},{13,25},{25,37},{37,1},{2,14}... | collective-permute-start | bytes 196616 | tf_op jit(solution)/shard_map/ppermute | solution.py:20
  10.5 7.4 %collective-permute-start.3 = (f32[128,128]{1,0:T(8,128)S(1)}, f32[128,128]{1,0:T(8,128)S(1)}, u32[]{:S(2)}, u32[]{:S(2)}) collective-permute-start(f32[128,128]{1,0:T(8,128)S(1)} %get-tuple-element.72.refs_3_), channel_id=1, source_target_pairs={{0,36},{12,0},{24,12},{36,24},{1,37},{13,1},{25,13},{37,25},{2,38}... | collective-permute-start | bytes 196616 | tf_op jit(solution)/shard_map/ppermute | solution.py:20
  17.9 1.9 %collective-permute-start = (f32[128,128]{1,0:T(8,128)S(1)}, f32[128,128]{1,0:T(8,128)S(1)}, u32[]{:S(2)}, u32[]{:S(2)}) collective-permute-start(f32[128,128]{1,0:T(8,128)S(1)} %get-tuple-element.73.refs_2_), channel_id=1, source_target_pairs={{0,48},{48,96},{96,144},{144,192},{192,240},{240,288},{288,336},{3... | collective-permute-start | bytes 196616 | tf_op jit(solution)/shard_map/ppermute | solution.py:20
  19.8 7.0 %collective-permute-start.1 = (f32[128,128]{1,0:T(8,128)S(1)}, f32[128,128]{1,0:T(8,128)S(1)}, u32[]{:S(2)}, u32[]{:S(2)}) collective-permute-start(f32[128,128]{1,0:T(8,128)S(1)} %get-tuple-element.74.refs_1_), channel_id=1, source_target_pairs={{0,720},{48,0},{96,48},{144,96},{192,144},{240,192},{288,240},{336... | collective-permute-start | bytes 196616 | tf_op jit(solution)/shard_map/ppermute | solution.py:20
  26.8 0.0 collective-permute-done.4.refs_11_
  26.8 6.7 %collective-permute-start.5 = (f32[128,128]{1,0:T(8,128)S(1)}, f32[128,128]{1,0:T(8,128)S(1)}, u32[]{:S(2)}, u32[]{:S(2)}) collective-permute-start(f32[128,128]{1,0:T(8,128)S(1)} %get-tuple-element.75.refs_5_), channel_id=1, source_target_pairs={{0,11},{1,0},{2,1},{3,2},{4,3},{5,4},{6,5},{7,6},{8,7},{9,8},{10,9... | collective-permute-start | bytes 196616 | tf_op jit(solution)/shard_map/ppermute | solution.py:20
  33.5 0.7 copy_bitcast_fusion
  34.3 1.3 copy-done
  35.5 0.8 reorder.2.refs_0_
  36.3 0.0 copy-start.1
  36.3 0.0 collective-permute-done.2.refs_9_
  36.3 0.0 collective-permute-done.3.refs_10_
  36.4 0.0 collective-permute-done.refs_7_
  36.4 0.0 collective-permute-done.1.refs_8_
  36.4 0.0 collective-permute-done.5.refs_12_
  36.4 0.5 product.4
  36.9 4.9 %collective-permute-start.7 = (f32[128,128]{1,0:T(8,128)S(1)}, f32[128,128]{1,0:T(8,128)S(1)}, u32[]{:S(2)}, u32[]{:S(2)}) collective-permute-start(f32[128,128]{1,0:T(8,128)S(1)} %get-tuple-element.37.refs_1_), channel_id=1, source_target_pairs={{0,720},{48,0},{96,48},{144,96},{192,144},{240,192},{288,240},{336... | collective-permute-start | bytes 196616 | tf_op jit(solution)/shard_map/ppermute | solution.py:20
  41.8 1.9 %collective-permute-start.6 = (f32[128,128]{1,0:T(8,128)S(1)}, f32[128,128]{1,0:T(8,128)S(1)}, u32[]{:S(2)}, u32[]{:S(2)}) collective-permute-start(f32[128,128]{1,0:T(8,128)S(1)} %get-tuple-element.38.refs_2_), channel_id=1, source_target_pairs={{0,48},{48,96},{96,144},{144,192},{192,240},{240,288},{288,336},{3... | collective-permute-start | bytes 196616 | tf_op jit(solution)/shard_map/ppermute | solution.py:20
  43.7 4.0 %collective-permute-start.9 = (f32[128,128]{1,0:T(8,128)S(1)}, f32[128,128]{1,0:T(8,128)S(1)}, u32[]{:S(2)}, u32[]{:S(2)}) collective-permute-start(f32[128,128]{1,0:T(8,128)S(1)} %get-tuple-element.39.refs_3_), channel_id=1, source_target_pairs={{0,36},{12,0},{24,12},{36,24},{1,37},{13,1},{25,13},{37,25},{2,38}... | collective-permute-start | bytes 196616 | tf_op jit(solution)/shard_map/ppermute | solution.py:20
  47.7 2.7 %collective-permute-start.8 = (f32[128,128]{1,0:T(8,128)S(1)}, f32[128,128]{1,0:T(8,128)S(1)}, u32[]{:S(2)}, u32[]{:S(2)}) collective-permute-start(f32[128,128]{1,0:T(8,128)S(1)} %get-tuple-element.40.refs_4_), channel_id=1, source_target_pairs={{0,12},{12,24},{24,36},{36,0},{1,13},{13,25},{25,37},{37,1},{2,14}... | collective-permute-start | bytes 196616 | tf_op jit(solution)/shard_map/ppermute | solution.py:20
  50.4 4.2 %collective-permute-start.11 = (f32[128,128]{1,0:T(8,128)S(1)}, f32[128,128]{1,0:T(8,128)S(1)}, u32[]{:S(2)}, u32[]{:S(2)}) collective-permute-start(f32[128,128]{1,0:T(8,128)S(1)} %get-tuple-element.41.refs_5_), channel_id=1, source_target_pairs={{0,11},{1,0},{2,1},{3,2},{4,3},{5,4},{6,5},{7,6},{8,7},{9,8},{10,9... | collective-permute-start | bytes 196616 | tf_op jit(solution)/shard_map/ppermute | solution.py:20
  54.6 0.0 collective-permute-done.7.refs_8_
  54.6 1.9 %collective-permute-start.10 = (f32[128,128]{1,0:T(8,128)S(1)}, f32[128,128]{1,0:T(8,128)S(1)}, u32[]{:S(2)}, u32[]{:S(2)}) collective-permute-start(f32[128,128]{1,0:T(8,128)S(1)} %get-tuple-element.42.refs_6_), channel_id=1, source_target_pairs={{0,1},{1,2},{2,3},{3,4},{4,5},{5,6},{6,7},{7,8},{8,9},{9,10},{10,1... | collective-permute-start | bytes 196616 | tf_op jit(solution)/shard_map/ppermute | solution.py:20
  56.6 0.8 reorder.3.refs_0_
  57.4 0.0 collective-permute-done.6.refs_7_
  57.4 0.0 collective-permute-done.9.refs_10_
  57.4 0.0 collective-permute-done.8.refs_9_
  57.4 0.0 collective-permute-done.11.refs_12_
  57.4 4.0 %collective-permute-done.10.refs_11_ = f32[128,128]{1,0:T(8,128)S(1)} collective-permute-done((f32[128,128]{1,0:T(8,128)S(1)}, f32[128,128]{1,0:T(8,128)S(1)}, u32[]{:S(2)}, u32[]{:S(2)}) %collective-permute-start.10) | collective-permute-done | bytes 65568 | tf_op jit(solution)/shard_map/ppermute | solution.py:20
  61.4 0.5 product.5
  61.9 7.3 %collective-permute-start.13 = (f32[128,128]{1,0:T(8,128)S(1)}, f32[128,128]{1,0:T(8,128)S(1)}, u32[]{:S(2)}, u32[]{:S(2)}) collective-permute-start(f32[128,128]{1,0:T(8,128)S(1)} %get-tuple-element.44.refs_1_), channel_id=1, source_target_pairs={{0,720},{48,0},{96,48},{144,96},{192,144},{240,192},{288,240},{336... | collective-permute-start | bytes 196616 | tf_op jit(solution)/shard_map/ppermute | solution.py:20
  69.2 1.9 %collective-permute-start.12 = (f32[128,128]{1,0:T(8,128)S(1)}, f32[128,128]{1,0:T(8,128)S(1)}, u32[]{:S(2)}, u32[]{:S(2)}) collective-permute-start(f32[128,128]{1,0:T(8,128)S(1)} %get-tuple-element.45.refs_2_), channel_id=1, source_target_pairs={{0,48},{48,96},{96,144},{144,192},{192,240},{240,288},{288,336},{3... | collective-permute-start | bytes 196616 | tf_op jit(solution)/shard_map/ppermute | solution.py:20
  71.1 3.0 %collective-permute-start.15 = (f32[128,128]{1,0:T(8,128)S(1)}, f32[128,128]{1,0:T(8,128)S(1)}, u32[]{:S(2)}, u32[]{:S(2)}) collective-permute-start(f32[128,128]{1,0:T(8,128)S(1)} %get-tuple-element.46.refs_3_), channel_id=1, source_target_pairs={{0,36},{12,0},{24,12},{36,24},{1,37},{13,1},{25,13},{37,25},{2,38}... | collective-permute-start | bytes 196616 | tf_op jit(solution)/shard_map/ppermute | solution.py:20
  74.2 2.5 %collective-permute-start.14 = (f32[128,128]{1,0:T(8,128)S(1)}, f32[128,128]{1,0:T(8,128)S(1)}, u32[]{:S(2)}, u32[]{:S(2)}) collective-permute-start(f32[128,128]{1,0:T(8,128)S(1)} %get-tuple-element.47.refs_4_), channel_id=1, source_target_pairs={{0,12},{12,24},{24,36},{36,0},{1,13},{13,25},{25,37},{37,1},{2,14}... | collective-permute-start | bytes 196616 | tf_op jit(solution)/shard_map/ppermute | solution.py:20
  76.7 1.9 %collective-permute-start.17 = (f32[128,128]{1,0:T(8,128)S(1)}, f32[128,128]{1,0:T(8,128)S(1)}, u32[]{:S(2)}, u32[]{:S(2)}) collective-permute-start(f32[128,128]{1,0:T(8,128)S(1)} %get-tuple-element.48.refs_5_), channel_id=1, source_target_pairs={{0,11},{1,0},{2,1},{3,2},{4,3},{5,4},{6,5},{7,6},{8,7},{9,8},{10,9... | collective-permute-start | bytes 196616 | tf_op jit(solution)/shard_map/ppermute | solution.py:20
  78.6 0.0 collective-permute-done.13.refs_8_
  78.6 3.4 %collective-permute-start.16 = (f32[128,128]{1,0:T(8,128)S(1)}, f32[128,128]{1,0:T(8,128)S(1)}, u32[]{:S(2)}, u32[]{:S(2)}) collective-permute-start(f32[128,128]{1,0:T(8,128)S(1)} %get-tuple-element.49.refs_6_), channel_id=1, source_target_pairs={{0,1},{1,2},{2,3},{3,4},{4,5},{5,6},{6,7},{7,8},{8,9},{9,10},{10,1... | collective-permute-start | bytes 196616 | tf_op jit(solution)/shard_map/ppermute | solution.py:20
  82.0 0.0 collective-permute-done.15.refs_10_
  82.0 0.0 collective-permute-done.14.refs_9_
  82.0 0.3 collective-permute-done.17.refs_12_
  82.4 3.1 %collective-permute-done.16.refs_11_ = f32[128,128]{1,0:T(8,128)S(1)} collective-permute-done((f32[128,128]{1,0:T(8,128)S(1)}, f32[128,128]{1,0:T(8,128)S(1)}, u32[]{:S(2)}, u32[]{:S(2)}) %collective-permute-start.16) | collective-permute-done | bytes 65568 | tf_op jit(solution)/shard_map/ppermute | solution.py:20
  85.5 0.5 product.6
  86.0 7.1 %collective-permute-start.19 = (f32[128,128]{1,0:T(8,128)S(1)}, f32[128,128]{1,0:T(8,128)S(1)}, u32[]{:S(2)}, u32[]{:S(2)}) collective-permute-start(f32[128,128]{1,0:T(8,128)S(1)} %get-tuple-element.51.refs_1_), channel_id=1, source_target_pairs={{0,720},{48,0},{96,48},{144,96},{192,144},{240,192},{288,240},{336... | collective-permute-start | bytes 196616 | tf_op jit(solution)/shard_map/ppermute | solution.py:20
  93.1 1.9 %collective-permute-start.18 = (f32[128,128]{1,0:T(8,128)S(1)}, f32[128,128]{1,0:T(8,128)S(1)}, u32[]{:S(2)}, u32[]{:S(2)}) collective-permute-start(f32[128,128]{1,0:T(8,128)S(1)} %get-tuple-element.52.refs_2_), channel_id=1, source_target_pairs={{0,48},{48,96},{96,144},{144,192},{192,240},{240,288},{288,336},{3... | collective-permute-start | bytes 196616 | tf_op jit(solution)/shard_map/ppermute | solution.py:20
  95.1 3.0 %collective-permute-start.21 = (f32[128,128]{1,0:T(8,128)S(1)}, f32[128,128]{1,0:T(8,128)S(1)}, u32[]{:S(2)}, u32[]{:S(2)}) collective-permute-start(f32[128,128]{1,0:T(8,128)S(1)} %get-tuple-element.53.refs_3_), channel_id=1, source_target_pairs={{0,36},{12,0},{24,12},{36,24},{1,37},{13,1},{25,13},{37,25},{2,38}... | collective-permute-start | bytes 196616 | tf_op jit(solution)/shard_map/ppermute | solution.py:20
  98.1 2.6 %collective-permute-start.20 = (f32[128,128]{1,0:T(8,128)S(1)}, f32[128,128]{1,0:T(8,128)S(1)}, u32[]{:S(2)}, u32[]{:S(2)}) collective-permute-start(f32[128,128]{1,0:T(8,128)S(1)} %get-tuple-element.54.refs_4_), channel_id=1, source_target_pairs={{0,12},{12,24},{24,36},{36,0},{1,13},{13,25},{25,37},{37,1},{2,14}... | collective-permute-start | bytes 196616 | tf_op jit(solution)/shard_map/ppermute | solution.py:20
  100.6 1.9 %collective-permute-start.23 = (f32[128,128]{1,0:T(8,128)S(1)}, f32[128,128]{1,0:T(8,128)S(1)}, u32[]{:S(2)}, u32[]{:S(2)}) collective-permute-start(f32[128,128]{1,0:T(8,128)S(1)} %get-tuple-element.55.refs_5_), channel_id=1, source_target_pairs={{0,11},{1,0},{2,1},{3,2},{4,3},{5,4},{6,5},{7,6},{8,7},{9,8},{10,9... | collective-permute-start | bytes 196616 | tf_op jit(solution)/shard_map/ppermute | solution.py:20
  102.6 3.4 %collective-permute-start.22 = (f32[128,128]{1,0:T(8,128)S(1)}, f32[128,128]{1,0:T(8,128)S(1)}, u32[]{:S(2)}, u32[]{:S(2)}) collective-permute-start(f32[128,128]{1,0:T(8,128)S(1)} %get-tuple-element.56.refs_6_), channel_id=1, source_target_pairs={{0,1},{1,2},{2,3},{3,4},{4,5},{5,6},{6,7},{7,8},{8,9},{9,10},{10,1... | collective-permute-start | bytes 196616 | tf_op jit(solution)/shard_map/ppermute | solution.py:20
  105.9 0.0 collective-permute-done.18.refs_7_
  106.0 0.3 collective-permute-done.23.refs_12_
  106.3 3.1 %collective-permute-done.22.refs_11_ = f32[128,128]{1,0:T(8,128)S(1)} collective-permute-done((f32[128,128]{1,0:T(8,128)S(1)}, f32[128,128]{1,0:T(8,128)S(1)}, u32[]{:S(2)}, u32[]{:S(2)}) %collective-permute-start.22) | collective-permute-done | bytes 65568 | tf_op jit(solution)/shard_map/ppermute | solution.py:20
  109.5 0.5 product.7
  110.0 0.7 broadcast_in_dim.8
  110.6 5.7 %all-to-all-start = ((f32[48,4,128]{2,1,0:T(4,128)}), f32[48,4,128]{2,1,0:T(4,128)S(1)}, u32[]{:S(2)}, u32[]{:S(2)}) async-start(f32[48,4,128]{2,1,0:T(4,128)} %broadcast_in_dim.8), calls=%async_computation | async-start | bytes 196608 | tf_op jit(solution)/shard_map/all_to_all | solution.py:159
  116.4 1.9 %collective-permute-start.24 = (f32[128,128]{1,0:T(8,128)S(1)}, f32[128,128]{1,0:T(8,128)S(1)}, u32[]{:S(2)}, u32[]{:S(2)}) collective-permute-start(f32[128,128]{1,0:T(8,128)S(1)} %get-tuple-element.65), channel_id=1, source_target_pairs={{0,48},{48,96},{96,144},{144,192},{192,240},{240,288},{288,336},{3... | collective-permute-start | bytes 196616 | tf_op jit(solution)/shard_map/ppermute | solution.py:20
  118.3 3.6 %collective-permute-start.25 = (f32[128,128]{1,0:T(8,128)S(1)}, f32[128,128]{1,0:T(8,128)S(1)}, u32[]{:S(2)}, u32[]{:S(2)}) collective-permute-start(f32[128,128]{1,0:T(8,128)S(1)} %get-tuple-element.66), channel_id=1, source_target_pairs={{0,12},{12,24},{24,36},{36,0},{1,13},{13,25},{25,37},{37,1},{2,14}... | collective-permute-start | bytes 196616 | tf_op jit(solution)/shard_map/ppermute | solution.py:20
  121.9 3.1 %collective-permute-start.26 = (f32[128,128]{1,0:T(8,128)S(1)}, f32[128,128]{1,0:T(8,128)S(1)}, u32[]{:S(2)}, u32[]{:S(2)}) collective-permute-start(f32[128,128]{1,0:T(8,128)S(1)} %get-tuple-element.67), channel_id=1, source_target_pairs={{0,1},{1,2},{2,3},{3,4},{4,5},{5,6},{6,7},{7,8},{8,9},{9,10},{10,1... | collective-permute-start | bytes 196616 | tf_op jit(solution)/shard_map/ppermute | solution.py:20
  125.0 4.0 %all-to-all-done = f32[48,4,128]{2,1,0:T(4,128)S(1)} async-done(((f32[48,4,128]{2,1,0:T(4,128)}), f32[48,4,128]{2,1,0:T(4,128)S(1)}, u32[]{:S(2)}, u32[]{:S(2)}) %all-to-all-start) | async-done | bytes 98336 | tf_op jit(solution)/shard_map/all_to_all | solution.py:159
  129.0 0.1 reduce_sum.18
  129.1 16.7 %all_to_all.10 = f32[16,4,128]{2,1,0:T(4,128)S(1)} all-to-all(f32[16,4,128]{2,1,0:T(4,128)S(1)} %broadcast_in_dim.9), channel_id=1, replica_groups=mesh['gx_0'=8,'gx_1'=2,'gy_0'=2,'gy_1'=2,'gz'=12] {'gx_0','gx_1'}, dimensions={0} | all-to-all | bytes 65536 | tf_op jit(solution)/shard_map/all_to_all | solution.py:159
  145.8 0.0 collective-permute-done.26.a4
  145.8 0.8 finish.1
  (11 shorter events, 0.1 us)
Async XLA Ops:
  1.7 25.2 %collective-permute-start.4 = (f32[128,128]{1,0:T(8,128)S(1)}, f32[128,128]{1,0:T(8,128)S(1)}, u32[]{:S(2)}, u32[]{:S(2)}) collective-permute-start(f32[128,128]{1,0:T(8,128)S(1)} %get-tuple-element.70.refs_6_), channel_id=1, source_target_pairs={{0,1},{1,2},{2,3},{3,4},{4,5},{5,6},{6,7},{7,8},{8,9},{9,10},{10,1... | collective-permute-start | bytes 196616 | tf_op jit(solution)/shard_map/ppermute | solution.py:20
  6.5 29.9 %collective-permute-start.2 = (f32[128,128]{1,0:T(8,128)S(1)}, f32[128,128]{1,0:T(8,128)S(1)}, u32[]{:S(2)}, u32[]{:S(2)}) collective-permute-start(f32[128,128]{1,0:T(8,128)S(1)} %get-tuple-element.71.refs_4_), channel_id=1, source_target_pairs={{0,12},{12,24},{24,36},{36,0},{1,13},{13,25},{25,37},{37,1},{2,14}... | collective-permute-start | bytes 196616 | tf_op jit(solution)/shard_map/ppermute | solution.py:20
  10.5 25.9 %collective-permute-start.3 = (f32[128,128]{1,0:T(8,128)S(1)}, f32[128,128]{1,0:T(8,128)S(1)}, u32[]{:S(2)}, u32[]{:S(2)}) collective-permute-start(f32[128,128]{1,0:T(8,128)S(1)} %get-tuple-element.72.refs_3_), channel_id=1, source_target_pairs={{0,36},{12,0},{24,12},{36,24},{1,37},{13,1},{25,13},{37,25},{2,38}... | collective-permute-start | bytes 196616 | tf_op jit(solution)/shard_map/ppermute | solution.py:20
  17.9 18.5 %collective-permute-start = (f32[128,128]{1,0:T(8,128)S(1)}, f32[128,128]{1,0:T(8,128)S(1)}, u32[]{:S(2)}, u32[]{:S(2)}) collective-permute-start(f32[128,128]{1,0:T(8,128)S(1)} %get-tuple-element.73.refs_2_), channel_id=1, source_target_pairs={{0,48},{48,96},{96,144},{144,192},{192,240},{240,288},{288,336},{3... | collective-permute-start | bytes 196616 | tf_op jit(solution)/shard_map/ppermute | solution.py:20
  19.8 16.5 %collective-permute-start.1 = (f32[128,128]{1,0:T(8,128)S(1)}, f32[128,128]{1,0:T(8,128)S(1)}, u32[]{:S(2)}, u32[]{:S(2)}) collective-permute-start(f32[128,128]{1,0:T(8,128)S(1)} %get-tuple-element.74.refs_1_), channel_id=1, source_target_pairs={{0,720},{48,0},{96,48},{144,96},{192,144},{240,192},{288,240},{336... | collective-permute-start | bytes 196616 | tf_op jit(solution)/shard_map/ppermute | solution.py:20
  26.8 9.6 %collective-permute-start.5 = (f32[128,128]{1,0:T(8,128)S(1)}, f32[128,128]{1,0:T(8,128)S(1)}, u32[]{:S(2)}, u32[]{:S(2)}) collective-permute-start(f32[128,128]{1,0:T(8,128)S(1)} %get-tuple-element.75.refs_5_), channel_id=1, source_target_pairs={{0,11},{1,0},{2,1},{3,2},{4,3},{5,4},{6,5},{7,6},{8,7},{9,8},{10,9... | collective-permute-start | bytes 196616 | tf_op jit(solution)/shard_map/ppermute | solution.py:20
  34.3 1.3 copy-start
  36.3 20.2 %copy-start.1 = (bf16[1,1,1,768,768]{4,3,2,1,0:T(8,128)(2,1)S(1)}, bf16[1,1,1,768,768]{4,3,2,1,0:T(8,128)(2,1)}, u32[]{:S(2)}) copy-start(bf16[1,1,1,768,768]{4,3,2,1,0:T(8,128)(2,1)} %param.5) | copy-start | bytes 3538948
  36.9 17.7 %collective-permute-start.7 = (f32[128,128]{1,0:T(8,128)S(1)}, f32[128,128]{1,0:T(8,128)S(1)}, u32[]{:S(2)}, u32[]{:S(2)}) collective-permute-start(f32[128,128]{1,0:T(8,128)S(1)} %get-tuple-element.37.refs_1_), channel_id=1, source_target_pairs={{0,720},{48,0},{96,48},{144,96},{192,144},{240,192},{288,240},{336... | collective-permute-start | bytes 196616 | tf_op jit(solution)/shard_map/ppermute | solution.py:20
  41.8 15.6 %collective-permute-start.6 = (f32[128,128]{1,0:T(8,128)S(1)}, f32[128,128]{1,0:T(8,128)S(1)}, u32[]{:S(2)}, u32[]{:S(2)}) collective-permute-start(f32[128,128]{1,0:T(8,128)S(1)} %get-tuple-element.38.refs_2_), channel_id=1, source_target_pairs={{0,48},{48,96},{96,144},{144,192},{192,240},{240,288},{288,336},{3... | collective-permute-start | bytes 196616 | tf_op jit(solution)/shard_map/ppermute | solution.py:20
  43.7 13.7 %collective-permute-start.9 = (f32[128,128]{1,0:T(8,128)S(1)}, f32[128,128]{1,0:T(8,128)S(1)}, u32[]{:S(2)}, u32[]{:S(2)}) collective-permute-start(f32[128,128]{1,0:T(8,128)S(1)} %get-tuple-element.39.refs_3_), channel_id=1, source_target_pairs={{0,36},{12,0},{24,12},{36,24},{1,37},{13,1},{25,13},{37,25},{2,38}... | collective-permute-start | bytes 196616 | tf_op jit(solution)/shard_map/ppermute | solution.py:20
  47.7 9.7 %collective-permute-start.8 = (f32[128,128]{1,0:T(8,128)S(1)}, f32[128,128]{1,0:T(8,128)S(1)}, u32[]{:S(2)}, u32[]{:S(2)}) collective-permute-start(f32[128,128]{1,0:T(8,128)S(1)} %get-tuple-element.40.refs_4_), channel_id=1, source_target_pairs={{0,12},{12,24},{24,36},{36,0},{1,13},{13,25},{25,37},{37,1},{2,14}... | collective-permute-start | bytes 196616 | tf_op jit(solution)/shard_map/ppermute | solution.py:20
  50.4 7.0 %collective-permute-start.11 = (f32[128,128]{1,0:T(8,128)S(1)}, f32[128,128]{1,0:T(8,128)S(1)}, u32[]{:S(2)}, u32[]{:S(2)}) collective-permute-start(f32[128,128]{1,0:T(8,128)S(1)} %get-tuple-element.41.refs_5_), channel_id=1, source_target_pairs={{0,11},{1,0},{2,1},{3,2},{4,3},{5,4},{6,5},{7,6},{8,7},{9,8},{10,9... | collective-permute-start | bytes 196616 | tf_op jit(solution)/shard_map/ppermute | solution.py:20
  54.6 6.8 %collective-permute-start.10 = (f32[128,128]{1,0:T(8,128)S(1)}, f32[128,128]{1,0:T(8,128)S(1)}, u32[]{:S(2)}, u32[]{:S(2)}) collective-permute-start(f32[128,128]{1,0:T(8,128)S(1)} %get-tuple-element.42.refs_6_), channel_id=1, source_target_pairs={{0,1},{1,2},{2,3},{3,4},{4,5},{5,6},{6,7},{7,8},{8,9},{9,10},{10,1... | collective-permute-start | bytes 196616 | tf_op jit(solution)/shard_map/ppermute | solution.py:20
  61.9 16.7 %collective-permute-start.13 = (f32[128,128]{1,0:T(8,128)S(1)}, f32[128,128]{1,0:T(8,128)S(1)}, u32[]{:S(2)}, u32[]{:S(2)}) collective-permute-start(f32[128,128]{1,0:T(8,128)S(1)} %get-tuple-element.44.refs_1_), channel_id=1, source_target_pairs={{0,720},{48,0},{96,48},{144,96},{192,144},{240,192},{288,240},{336... | collective-permute-start | bytes 196616 | tf_op jit(solution)/shard_map/ppermute | solution.py:20
  69.2 12.8 %collective-permute-start.12 = (f32[128,128]{1,0:T(8,128)S(1)}, f32[128,128]{1,0:T(8,128)S(1)}, u32[]{:S(2)}, u32[]{:S(2)}) collective-permute-start(f32[128,128]{1,0:T(8,128)S(1)} %get-tuple-element.45.refs_2_), channel_id=1, source_target_pairs={{0,48},{48,96},{96,144},{144,192},{192,240},{240,288},{288,336},{3... | collective-permute-start | bytes 196616 | tf_op jit(solution)/shard_map/ppermute | solution.py:20
  71.1 10.9 %collective-permute-start.15 = (f32[128,128]{1,0:T(8,128)S(1)}, f32[128,128]{1,0:T(8,128)S(1)}, u32[]{:S(2)}, u32[]{:S(2)}) collective-permute-start(f32[128,128]{1,0:T(8,128)S(1)} %get-tuple-element.46.refs_3_), channel_id=1, source_target_pairs={{0,36},{12,0},{24,12},{36,24},{1,37},{13,1},{25,13},{37,25},{2,38}... | collective-permute-start | bytes 196616 | tf_op jit(solution)/shard_map/ppermute | solution.py:20
  74.2 7.9 %collective-permute-start.14 = (f32[128,128]{1,0:T(8,128)S(1)}, f32[128,128]{1,0:T(8,128)S(1)}, u32[]{:S(2)}, u32[]{:S(2)}) collective-permute-start(f32[128,128]{1,0:T(8,128)S(1)} %get-tuple-element.47.refs_4_), channel_id=1, source_target_pairs={{0,12},{12,24},{24,36},{36,0},{1,13},{13,25},{25,37},{37,1},{2,14}... | collective-permute-start | bytes 196616 | tf_op jit(solution)/shard_map/ppermute | solution.py:20
  76.7 5.7 %collective-permute-start.17 = (f32[128,128]{1,0:T(8,128)S(1)}, f32[128,128]{1,0:T(8,128)S(1)}, u32[]{:S(2)}, u32[]{:S(2)}) collective-permute-start(f32[128,128]{1,0:T(8,128)S(1)} %get-tuple-element.48.refs_5_), channel_id=1, source_target_pairs={{0,11},{1,0},{2,1},{3,2},{4,3},{5,4},{6,5},{7,6},{8,7},{9,8},{10,9... | collective-permute-start | bytes 196616 | tf_op jit(solution)/shard_map/ppermute | solution.py:20
  78.6 6.9 %collective-permute-start.16 = (f32[128,128]{1,0:T(8,128)S(1)}, f32[128,128]{1,0:T(8,128)S(1)}, u32[]{:S(2)}, u32[]{:S(2)}) collective-permute-start(f32[128,128]{1,0:T(8,128)S(1)} %get-tuple-element.49.refs_6_), channel_id=1, source_target_pairs={{0,1},{1,2},{2,3},{3,4},{4,5},{5,6},{6,7},{7,8},{8,9},{9,10},{10,1... | collective-permute-start | bytes 196616 | tf_op jit(solution)/shard_map/ppermute | solution.py:20
  86.0 16.6 %collective-permute-start.19 = (f32[128,128]{1,0:T(8,128)S(1)}, f32[128,128]{1,0:T(8,128)S(1)}, u32[]{:S(2)}, u32[]{:S(2)}) collective-permute-start(f32[128,128]{1,0:T(8,128)S(1)} %get-tuple-element.51.refs_1_), channel_id=1, source_target_pairs={{0,720},{48,0},{96,48},{144,96},{192,144},{240,192},{288,240},{336... | collective-permute-start | bytes 196616 | tf_op jit(solution)/shard_map/ppermute | solution.py:20
  93.1 12.8 %collective-permute-start.18 = (f32[128,128]{1,0:T(8,128)S(1)}, f32[128,128]{1,0:T(8,128)S(1)}, u32[]{:S(2)}, u32[]{:S(2)}) collective-permute-start(f32[128,128]{1,0:T(8,128)S(1)} %get-tuple-element.52.refs_2_), channel_id=1, source_target_pairs={{0,48},{48,96},{96,144},{144,192},{192,240},{240,288},{288,336},{3... | collective-permute-start | bytes 196616 | tf_op jit(solution)/shard_map/ppermute | solution.py:20
  95.1 10.9 %collective-permute-start.21 = (f32[128,128]{1,0:T(8,128)S(1)}, f32[128,128]{1,0:T(8,128)S(1)}, u32[]{:S(2)}, u32[]{:S(2)}) collective-permute-start(f32[128,128]{1,0:T(8,128)S(1)} %get-tuple-element.53.refs_3_), channel_id=1, source_target_pairs={{0,36},{12,0},{24,12},{36,24},{1,37},{13,1},{25,13},{37,25},{2,38}... | collective-permute-start | bytes 196616 | tf_op jit(solution)/shard_map/ppermute | solution.py:20
  98.1 7.9 %collective-permute-start.20 = (f32[128,128]{1,0:T(8,128)S(1)}, f32[128,128]{1,0:T(8,128)S(1)}, u32[]{:S(2)}, u32[]{:S(2)}) collective-permute-start(f32[128,128]{1,0:T(8,128)S(1)} %get-tuple-element.54.refs_4_), channel_id=1, source_target_pairs={{0,12},{12,24},{24,36},{36,0},{1,13},{13,25},{25,37},{37,1},{2,14}... | collective-permute-start | bytes 196616 | tf_op jit(solution)/shard_map/ppermute | solution.py:20
  100.6 5.7 %collective-permute-start.23 = (f32[128,128]{1,0:T(8,128)S(1)}, f32[128,128]{1,0:T(8,128)S(1)}, u32[]{:S(2)}, u32[]{:S(2)}) collective-permute-start(f32[128,128]{1,0:T(8,128)S(1)} %get-tuple-element.55.refs_5_), channel_id=1, source_target_pairs={{0,11},{1,0},{2,1},{3,2},{4,3},{5,4},{6,5},{7,6},{8,7},{9,8},{10,9... | collective-permute-start | bytes 196616 | tf_op jit(solution)/shard_map/ppermute | solution.py:20
  102.6 6.9 %collective-permute-start.22 = (f32[128,128]{1,0:T(8,128)S(1)}, f32[128,128]{1,0:T(8,128)S(1)}, u32[]{:S(2)}, u32[]{:S(2)}) collective-permute-start(f32[128,128]{1,0:T(8,128)S(1)} %get-tuple-element.56.refs_6_), channel_id=1, source_target_pairs={{0,1},{1,2},{2,3},{3,4},{4,5},{5,6},{6,7},{7,8},{8,9},{9,10},{10,1... | collective-permute-start | bytes 196616 | tf_op jit(solution)/shard_map/ppermute | solution.py:20
  110.6 18.3 %all-to-all-start = ((f32[48,4,128]{2,1,0:T(4,128)}), f32[48,4,128]{2,1,0:T(4,128)S(1)}, u32[]{:S(2)}, u32[]{:S(2)}) async-start(f32[48,4,128]{2,1,0:T(4,128)} %broadcast_in_dim.8), calls=%async_computation | async-start | bytes 196608 | tf_op jit(solution)/shard_map/all_to_all | solution.py:159
  116.4 29.5 %collective-permute-start.24 = (f32[128,128]{1,0:T(8,128)S(1)}, f32[128,128]{1,0:T(8,128)S(1)}, u32[]{:S(2)}, u32[]{:S(2)}) collective-permute-start(f32[128,128]{1,0:T(8,128)S(1)} %get-tuple-element.65), channel_id=1, source_target_pairs={{0,48},{48,96},{96,144},{144,192},{192,240},{240,288},{288,336},{3... | collective-permute-start | bytes 196616 | tf_op jit(solution)/shard_map/ppermute | solution.py:20
  118.3 27.5 %collective-permute-start.25 = (f32[128,128]{1,0:T(8,128)S(1)}, f32[128,128]{1,0:T(8,128)S(1)}, u32[]{:S(2)}, u32[]{:S(2)}) collective-permute-start(f32[128,128]{1,0:T(8,128)S(1)} %get-tuple-element.66), channel_id=1, source_target_pairs={{0,12},{12,24},{24,36},{36,0},{1,13},{13,25},{25,37},{37,1},{2,14}... | collective-permute-start | bytes 196616 | tf_op jit(solution)/shard_map/ppermute | solution.py:20
  121.9 24.0 %collective-permute-start.26 = (f32[128,128]{1,0:T(8,128)S(1)}, f32[128,128]{1,0:T(8,128)S(1)}, u32[]{:S(2)}, u32[]{:S(2)}) collective-permute-start(f32[128,128]{1,0:T(8,128)S(1)} %get-tuple-element.67), channel_id=1, source_target_pairs={{0,1},{1,2},{2,3},{3,4},{4,5},{5,6},{6,7},{7,8},{8,9},{9,10},{10,1... | collective-permute-start | bytes 196616 | tf_op jit(solution)/shard_map/ppermute | solution.py:20
